TPU v7x, 32 devices: a whole 2x2x4 slice. The times are simulated.
32 devices in a mesh: fsdp: 8 (over y, x, core), seq: 4 (over z).
Axes of the slice: x: 2, y: 2, z: 4, core: 2. Of those that a mesh axis runs over, the one named last changes fastest.
Arguments:
- hidden_in: bfloat16 [8, 1024, 2048], P('fsdp', 'seq'), may hold values from -6 to 6
- lengths: int32 [8], P('fsdp'), may hold values from 512 to 1024, as said below
- cotangent: bfloat16 [8, 1024, 2048], P('fsdp', 'seq'), may hold values from -6 to 6
- in_weight: bfloat16 [2048, 6144], P(('fsdp', 'seq')), may hold values from -0.125 to 0.125
- in_bias: bfloat16 [6144], P(('fsdp', 'seq')), may hold values from -0.29882812 to 0.29882812
- out_weight: bfloat16 [2048, 2048], P(('fsdp', 'seq')), may hold values from -1 to 1
- out_bias: bfloat16 [2048], P(('fsdp', 'seq')), may hold values from -2 to 2
- up_weight: bfloat16 [8192, 2048], P(('fsdp', 'seq')), may hold values from -0.125 to 0.125
- up_bias: bfloat16 [8192], P(('fsdp', 'seq')), may hold values from -2 to 2
- down_weight: bfloat16 [8192, 2048], P(('fsdp', 'seq')), may hold values from -0.0625 to 0.0625
- down_bias: bfloat16 [2048], P(('fsdp', 'seq')), may hold values from -2 to 2
- first_gain: bfloat16 [2048], P(('fsdp', 'seq')), may hold values from 0.5 to 1.5
- first_shift: bfloat16 [2048], P(('fsdp', 'seq')), may hold values from -2 to 2
- second_gain: bfloat16 [2048], P(('fsdp', 'seq')), may hold values from 0.5 to 1.5
- second_shift: bfloat16 [2048], P(('fsdp', 'seq')), may hold values from -2 to 2
Outputs:
- layer_output: float32 [8, 1024, 2048], P('fsdp', 'seq')
- input_gradient: float32 [8, 1024, 2048], P('fsdp', 'seq')
- in_weight_gradient: float32 [2048, 6144], P(('fsdp', 'seq'))
- in_bias_gradient: float32 [6144], P(('fsdp', 'seq'))
- out_weight_gradient: float32 [2048, 2048], P(('fsdp', 'seq'))
- out_bias_gradient: float32 [2048], P(('fsdp', 'seq'))
- up_weight_gradient: float32 [8192, 2048], P(('fsdp', 'seq'))
- up_bias_gradient: float32 [8192], P(('fsdp', 'seq'))
- down_weight_gradient: float32 [8192, 2048], P(('fsdp', 'seq'))
- down_bias_gradient: float32 [2048], P(('fsdp', 'seq'))
- first_gain_gradient: float32 [2048], P(('fsdp', 'seq'))
- first_shift_gradient: float32 [2048], P(('fsdp', 'seq'))
- second_gain_gradient: float32 [2048], P(('fsdp', 'seq'))
- second_shift_gradient: float32 [2048], P(('fsdp', 'seq'))
Inputs may be any that keep to these rules, and one draw needn't show every extreme that they name: `lengths`: tokens in use at the front of each slot; in every draw one slot is full and one holds 512 tokens.
All inputs are finite; a program needn't handle non-finite values.
Results may differ from a plain program's by a relative error of at most 0.014.
Values may be sent and summed in bfloat16 or wider, within the bound.
No kernel may reach another device: no remote copies, remote signals or barrier semaphores. Data moves between devices by JAX's collectives and lax.ppermute only.
A program may use at most 384 MiB of HBM per device.

v0:
```python
import jax
import jax.numpy as jnp
from jax import lax
from jax.sharding import PartitionSpec as P

HEADS = 16
HEAD_DIM = 128
ROT = 32
EPSILON = 1e-05
MASKED_SCORE = -1e30


def layer_norm(values, norm_gain, norm_shift):
    centred = values - jnp.mean(values, axis=-1, keepdims=True)
    spread = jnp.mean(centred * centred, axis=-1, keepdims=True)
    return centred * lax.rsqrt(spread + EPSILON) * norm_gain + norm_shift


def rotary_tables(positions):
    halves = jnp.arange(ROT // 2, dtype=jnp.float32)
    frequency = 1.0 / 10000.0 ** (halves * 2.0 / ROT)
    angles = positions.astype(jnp.float32)[:, None] * frequency[None, :]
    angles = jnp.concatenate([angles, angles], axis=1)
    return (jnp.cos(angles), jnp.sin(angles))


def rotate(values, cosine_table, sine_table):
    leading = values[..., :ROT]
    middle = ROT // 2
    turned = jnp.concatenate([-leading[..., middle:], leading[..., :middle]], axis=-1)
    leading = leading * cosine_table[:, None, :] + turned * sine_table[:, None, :]
    return jnp.concatenate([leading, values[..., ROT:]], axis=-1)


def exact_gelu(values):
    return jax.nn.gelu(values, approximate=False)


def matmul(left_side, right_side):
    return jnp.dot(left_side, right_side, preferred_element_type=jnp.float32)


def times_transposed(left_side, right_side):
    return lax.dot_general(
        left_side, right_side, (((1,), (1,)), ((), ())), preferred_element_type=jnp.float32
    )


def transposed_times(left_side, right_side):
    return lax.dot_general(
        left_side, right_side, (((0,), (0,)), ((), ())), preferred_element_type=jnp.float32
    )


def attend_slot(query, key_rows, value_rows, keep_mask):
    length_full = query.shape[0]
    block_rows = min(512, length_full)
    block_count = length_full // block_rows
    columns = jnp.arange(length_full, dtype=jnp.int32)
    scale_factor = HEAD_DIM ** (-0.5)

    def one_block(first_row):
        row_index = first_row + jnp.arange(block_rows, dtype=jnp.int32)
        query_block = lax.dynamic_slice_in_dim(query, first_row, block_rows, 0)
        scores = (
            jnp.einsum("qhd,khd->hqk", query_block, key_rows, preferred_element_type=jnp.float32)
            * scale_factor
        )
        allowed = (columns[None, :] <= row_index[:, None]) & keep_mask[None, :]
        scores = jnp.where(allowed[None], scores, MASKED_SCORE)
        largest = jnp.max(scores, axis=-1, keepdims=True)
        weights = jnp.exp(scores - largest)
        totals = jnp.sum(weights, axis=-1, keepdims=True)
        probabilities = (weights / totals).astype(jnp.bfloat16)
        mixed = jnp.einsum(
            "hqk,khd->qhd", probabilities, value_rows, preferred_element_type=jnp.float32
        )
        return (mixed, (largest + jnp.log(totals))[..., 0])

    starts = jnp.arange(block_count, dtype=jnp.int32) * block_rows
    mixed, log_sums = lax.map(one_block, starts)
    return (mixed.reshape(length_full, query.shape[1], query.shape[2]), log_sums)


def attend_slot_back(query, key_rows, value_rows, keep_mask, log_sums, mixed_delta):
    length_full = query.shape[0]
    block_rows = min(512, length_full)
    block_count = length_full // block_rows
    columns = jnp.arange(length_full, dtype=jnp.int32)
    scale_factor = HEAD_DIM ** (-0.5)

    def one_block(carried, member):
        key_delta, value_delta = carried
        first_row, log_block = member
        row_index = first_row + jnp.arange(block_rows, dtype=jnp.int32)
        query_block = lax.dynamic_slice_in_dim(query, first_row, block_rows, 0)
        delta_block = lax.dynamic_slice_in_dim(mixed_delta, first_row, block_rows, 0)
        scores = (
            jnp.einsum("qhd,khd->hqk", query_block, key_rows, preferred_element_type=jnp.float32)
            * scale_factor
        )
        allowed = (columns[None, :] <= row_index[:, None]) & keep_mask[None, :]
        scores = jnp.where(allowed[None], scores, MASKED_SCORE)
        probabilities = jnp.where(allowed[None], jnp.exp(scores - log_block[..., None]), 0.0)
        prob_delta = jnp.einsum(
            "qhd,khd->hqk", delta_block, value_rows, preferred_element_type=jnp.float32
        )
        row_dot = jnp.sum(probabilities * prob_delta, axis=-1, keepdims=True)
        score_delta = (probabilities * (prob_delta - row_dot)).astype(jnp.bfloat16)
        query_delta = (
            jnp.einsum("hqk,khd->qhd", score_delta, key_rows, preferred_element_type=jnp.float32)
            * scale_factor
        )
        key_delta = (
            key_delta
            + jnp.einsum(
                "hqk,qhd->khd", score_delta, query_block, preferred_element_type=jnp.float32
            )
            * scale_factor
        )
        value_delta = value_delta + jnp.einsum(
            "hqk,qhd->khd",
            probabilities.astype(jnp.bfloat16),
            delta_block,
            preferred_element_type=jnp.float32,
        )
        return ((key_delta, value_delta), query_delta)

    starts = jnp.arange(block_count, dtype=jnp.int32) * block_rows
    zeroes = jnp.zeros(query.shape, jnp.float32)
    (key_delta, value_delta), query_delta = lax.scan(
        one_block, (zeroes, zeroes), (starts, log_sums)
    )
    return (query_delta.reshape(query.shape), key_delta, value_delta)


def feed_forward(inner_in, up_matrix, up_offset, down_matrix):
    hidden_pre = times_transposed(inner_in, up_matrix) + up_offset.astype(jnp.float32)
    hidden_act, pull_act = jax.vjp(exact_gelu, hidden_pre)
    hidden_low = hidden_act.astype(jnp.bfloat16)
    return (hidden_low, pull_act, matmul(hidden_low, down_matrix))


def feed_back(inner_in, hidden_low, pull_act, delta_rows, up_matrix, down_matrix):
    delta_down = transposed_times(hidden_low, delta_rows)
    delta_pre = pull_act(times_transposed(delta_rows, down_matrix))[0].astype(jnp.bfloat16)
    delta_up = transposed_times(delta_pre, inner_in)
    delta_up_bias = jnp.sum(delta_pre.astype(jnp.float32), axis=0)
    delta_inner = matmul(delta_pre, up_matrix)
    return (delta_up, delta_up_bias, delta_down, delta_inner)


def local(
    hidden_in,
    lengths,
    cotangent,
    in_weight,
    in_bias,
    out_weight,
    out_bias,
    up_weight,
    up_bias,
    down_weight,
    down_bias,
    first_gain,
    first_shift,
    second_gain,
    second_shift,
):
    slot_count, token_count, width = hidden_in.shape
    seq_count = lax.axis_size("seq")
    seq_index = lax.axis_index("seq")
    length_full = token_count * seq_count
    row_count = slot_count * token_count
    (
        in_matrix,
        in_offset,
        out_matrix,
        out_offset,
        gain_one,
        shift_one,
        gain_two,
        shift_two,
        down_offset,
    ) = (
        lax.all_gather(in_weight, ("fsdp", "seq"), axis=0, tiled=True),
        lax.all_gather(in_bias, ("fsdp", "seq"), axis=0, tiled=True),
        lax.all_gather(out_weight, ("fsdp", "seq"), axis=0, tiled=True),
        lax.all_gather(out_bias, ("fsdp", "seq"), axis=0, tiled=True),
        lax.all_gather(first_gain, ("fsdp", "seq"), axis=0, tiled=True),
        lax.all_gather(first_shift, ("fsdp", "seq"), axis=0, tiled=True),
        lax.all_gather(second_gain, ("fsdp", "seq"), axis=0, tiled=True),
        lax.all_gather(second_shift, ("fsdp", "seq"), axis=0, tiled=True),
        lax.all_gather(down_bias, ("fsdp", "seq"), axis=0, tiled=True),
    )
    positions = seq_index * token_count + jnp.arange(token_count, dtype=jnp.int32)
    keep_local = positions[None, :] < lengths[:, None]
    keep_full = jnp.arange(length_full, dtype=jnp.int32)[None, :] < lengths[:, None]
    source = hidden_in.astype(jnp.float32)
    normed_one, pull_one = jax.vjp(
        layer_norm, source, gain_one.astype(jnp.float32), shift_one.astype(jnp.float32)
    )
    first_in = normed_one.astype(jnp.bfloat16).reshape(row_count, width)
    cosine_table, sine_table = rotary_tables(positions)
    joined = matmul(first_in, in_matrix) + in_offset.astype(jnp.float32)
    joined = joined.reshape(slot_count, token_count, 3, HEADS, HEAD_DIM)

    def rotate_both(query_part, key_part):
        return (
            rotate(query_part, cosine_table, sine_table),
            rotate(key_part, cosine_table, sine_table),
        )

    turned, pull_turn = jax.vjp(rotate_both, joined[:, :, 0], joined[:, :, 1])
    query, key_rows, value_rows = (
        lax.all_to_all(
            turned[0].astype(jnp.bfloat16), "seq", split_axis=2, concat_axis=1, tiled=True
        ),
        lax.all_to_all(
            turned[1].astype(jnp.bfloat16), "seq", split_axis=2, concat_axis=1, tiled=True
        ),
        lax.all_to_all(
            joined[:, :, 2].astype(jnp.bfloat16), "seq", split_axis=2, concat_axis=1, tiled=True
        ),
    )
    mixed_heads, log_sums = jax.vmap(attend_slot)(query, key_rows, value_rows, keep_full)
    mixed = lax.all_to_all(
        mixed_heads.astype(jnp.bfloat16), "seq", split_axis=1, concat_axis=2, tiled=True
    ).reshape(row_count, width)
    attn_branch = matmul(mixed, out_matrix) + out_offset.astype(jnp.float32)
    normed_two, pull_two = jax.vjp(
        layer_norm, source, gain_two.astype(jnp.float32), shift_two.astype(jnp.float32)
    )
    second_in = normed_two.astype(jnp.bfloat16)
    delta_out = jnp.where(keep_local[..., None], cotangent.astype(jnp.float32), 0.0)
    delta_low = delta_out.astype(jnp.bfloat16)
    delta_rows = delta_low.reshape(row_count, width)
    up_matrix, up_offset, down_matrix = (
        lax.all_gather(up_weight, "fsdp", axis=0, tiled=True),
        lax.all_gather(up_bias, "fsdp", axis=0, tiled=True),
        lax.all_gather(down_weight, "fsdp", axis=0, tiled=True),
    )
    inner_in = lax.all_gather(second_in, "seq", axis=1, tiled=True).reshape(
        slot_count * length_full, width
    )
    hidden_low, pull_act, branch_part = feed_forward(inner_in, up_matrix, up_offset, down_matrix)
    branch_sum = lax.psum_scatter(
        branch_part.reshape(slot_count, length_full, width).astype(jnp.bfloat16),
        "seq",
        scatter_dimension=1,
        tiled=True,
    ).astype(jnp.float32)
    mlp_branch = branch_sum + down_offset.astype(jnp.float32)
    delta_all = lax.all_gather(delta_low, "seq", axis=1, tiled=True).reshape(
        slot_count * length_full, width
    )
    delta_up, delta_up_bias, delta_down, delta_inner = feed_back(
        inner_in, hidden_low, pull_act, delta_all, up_matrix, down_matrix
    )
    second_delta = lax.psum_scatter(
        delta_inner.reshape(slot_count, length_full, width).astype(jnp.bfloat16),
        "seq",
        scatter_dimension=1,
        tiled=True,
    ).astype(jnp.float32)
    up_gradient, up_bias_gradient, down_gradient = (
        lax.psum_scatter(
            delta_up.astype(jnp.bfloat16), "fsdp", scatter_dimension=0, tiled=True
        ).astype(jnp.float32),
        lax.psum_scatter(
            delta_up_bias.astype(jnp.bfloat16), "fsdp", scatter_dimension=0, tiled=True
        ).astype(jnp.float32),
        lax.psum_scatter(
            delta_down.astype(jnp.bfloat16), "fsdp", scatter_dimension=0, tiled=True
        ).astype(jnp.float32),
    )
    layer_output = jnp.where(
        keep_local[..., None],
        source + attn_branch.reshape(slot_count, token_count, width) + mlp_branch,
        0.0,
    )
    source_two, gain_two_delta, shift_two_delta = pull_two(second_delta)
    bias_sum = jnp.sum(delta_out.reshape(row_count, width), axis=0)
    out_delta = transposed_times(mixed, delta_rows)
    mixed_delta = times_transposed(delta_rows, out_matrix).astype(jnp.bfloat16)
    mixed_delta = lax.all_to_all(
        mixed_delta.reshape(slot_count, token_count, HEADS, HEAD_DIM),
        "seq",
        split_axis=2,
        concat_axis=1,
        tiled=True,
    )
    query_delta, key_delta, value_delta = jax.vmap(attend_slot_back)(
        query, key_rows, value_rows, keep_full, log_sums, mixed_delta
    )
    query_back, key_back, value_back = (
        lax.all_to_all(
            query_delta.astype(jnp.bfloat16), "seq", split_axis=1, concat_axis=2, tiled=True
        ),
        lax.all_to_all(
            key_delta.astype(jnp.bfloat16), "seq", split_axis=1, concat_axis=2, tiled=True
        ),
        lax.all_to_all(
            value_delta.astype(jnp.bfloat16), "seq", split_axis=1, concat_axis=2, tiled=True
        ),
    )
    query_plain, key_plain = pull_turn(
        (query_back.astype(jnp.float32), key_back.astype(jnp.float32))
    )
    joined_delta = jnp.stack([query_plain, key_plain, value_back.astype(jnp.float32)], axis=2)
    joined_delta = joined_delta.reshape(row_count, 3 * width).astype(jnp.bfloat16)
    in_delta = transposed_times(first_in, joined_delta)
    in_bias_delta = jnp.sum(joined_delta.astype(jnp.float32), axis=0)
    first_delta = times_transposed(joined_delta, in_matrix).reshape(slot_count, token_count, width)
    source_one, gain_one_delta, shift_one_delta = pull_one(first_delta)
    (
        in_gradient,
        in_bias_gradient,
        out_gradient,
        bias_gradient,
        gain_one_gradient,
        shift_one_gradient,
        gain_two_gradient,
        shift_two_gradient,
    ) = (
        lax.psum_scatter(in_delta, ("fsdp", "seq"), scatter_dimension=0, tiled=True),
        lax.psum_scatter(in_bias_delta, ("fsdp", "seq"), scatter_dimension=0, tiled=True),
        lax.psum_scatter(out_delta, ("fsdp", "seq"), scatter_dimension=0, tiled=True),
        lax.psum_scatter(bias_sum, ("fsdp", "seq"), scatter_dimension=0, tiled=True),
        lax.psum_scatter(gain_one_delta, ("fsdp", "seq"), scatter_dimension=0, tiled=True),
        lax.psum_scatter(shift_one_delta, ("fsdp", "seq"), scatter_dimension=0, tiled=True),
        lax.psum_scatter(gain_two_delta, ("fsdp", "seq"), scatter_dimension=0, tiled=True),
        lax.psum_scatter(shift_two_delta, ("fsdp", "seq"), scatter_dimension=0, tiled=True),
    )
    input_gradient = delta_out + source_one + source_two
    return (
        layer_output,
        input_gradient,
        in_gradient,
        in_bias_gradient,
        out_gradient,
        bias_gradient,
        up_gradient,
        up_bias_gradient,
        down_gradient,
        bias_gradient,
        gain_one_gradient,
        shift_one_gradient,
        gain_two_gradient,
        shift_two_gradient,
    )


def solution(mesh):
    return jax.shard_map(
        local,
        mesh=mesh,
        in_specs=(
            P("fsdp", "seq", None),
            P("fsdp"),
            P("fsdp", "seq", None),
            P(("fsdp", "seq"), None),
            P(("fsdp", "seq")),
            P(("fsdp", "seq"), None),
            P(("fsdp", "seq")),
            P(("fsdp", "seq"), None),
            P(("fsdp", "seq")),
            P(("fsdp", "seq"), None),
            P(("fsdp", "seq")),
            P(("fsdp", "seq")),
            P(("fsdp", "seq")),
            P(("fsdp", "seq")),
            P(("fsdp", "seq")),
        ),
        out_specs=(
            P("fsdp", "seq", None),
            P("fsdp", "seq", None),
            P(("fsdp", "seq"), None),
            P(("fsdp", "seq")),
            P(("fsdp", "seq"), None),
            P(("fsdp", "seq")),
            P(("fsdp", "seq"), None),
            P(("fsdp", "seq")),
            P(("fsdp", "seq"), None),
            P(("fsdp", "seq")),
            P(("fsdp", "seq")),
            P(("fsdp", "seq")),
            P(("fsdp", "seq")),
            P(("fsdp", "seq")),
        ),
        check_vma=False,
    )
```

profile of v0, /device:TPU:0, one launch (start us, length us, event | category | flops | bytes accessed | tf_op | source)
XLA Modules:
  0.0 1959.2 jit_solution(5670677345125691977)
XLA Ops:
  16.4 43.3 %all-reduce.25 = (bf16[6144]{0:T(1024)(128)(2,1)S(1)}, bf16[2048]{0:T(1024)(128)(2,1)S(1)}, bf16[2048]{0:T(1024)(128)(2,1)S(1)}, bf16[2048]{0:T(1024)(128)(2,1)S...) all-reduce(bf16[6144]{0:T(1024)(128)(2,1)S(1)} %dynamic-update-slic, ...), channel_id=1, replica_groups=mesh['fsdp'=8,'seq'=4] {'fsdp','seq'}, use_global_device_ids=true, to_apply=%add.12 | all-reduce | flops 18432 | bytes 73728
  76.8 66.3 %all-gather.12.cloned.1.call-done = bf16[1,1024,2048]{2,1,0:T(8,128)(2,1)} async-done(((bf16[1,256,2048]{2,1,0:T(8,128)(2,1)}), bf16[1,1024,2048]{2,1,0:T(8,128)(2,1)}) %all-gather.12.cloned.1.call-update) | async-done | bytes 4194320 | tf_op jit(solution)/shard_map/all_gather | solution.py:243
  143.0 54.8 %all-gather.14.cloned.1.call-done = bf16[2048,2048]{1,0:T(8,128)(2,1)} async-done(((bf16[256,2048]{1,0:T(8,128)(2,1)}), bf16[2048,2048]{1,0:T(8,128)(2,1)}) %all-gather.14.cloned.1.call-update) | async-done | bytes 8388624 | tf_op jit(solution)/shard_map/all_gather | solution.py:239
  197.9 31.6 %multiply_convert_fusion.1 = (bf16[1024,2048]{1,0:T(8,128)(2,1)}, f32[1024,2048]{1,0:T(8,128)}, f32[1024,2048]{1,0:T(8,128)}) fusion(f32[2048]{0:T(1024)S(1)} %bitcast.299, bf16[2048,2048]{1,0:T(8,128)(2,1)} %all-gather.14.cloned.1.call-done, bf16[1,1024,2048]{2,1,0:T(8,128)(2,1)} %all-gather.12.cloned.1.call-done), kind=kOutput, calls=%fused_computation.61 | convolution fusion | flops 8728346624 | bytes 33562624 | tf_op jit(solution)/shard_map/dot_general | solution.py:44
  229.5 50.8 %all-gather.18.cloned.1.call-done = bf16[1,1024,2048]{2,1,0:T(8,128)(2,1)} async-done(((bf16[1,256,2048]{2,1,0:T(8,128)(2,1)}), bf16[1,1024,2048]{2,1,0:T(8,128)(2,1)}) %all-gather.18.cloned.1.call-update) | async-done | bytes 4194320 | tf_op jit(solution)/shard_map/all_gather | solution.py:254
  280.3 54.7 %all-gather.16.cloned.1.call-done = bf16[2048,2048]{1,0:T(8,128)(2,1)} async-done(((bf16[256,2048]{1,0:T(8,128)(2,1)}), bf16[2048,2048]{1,0:T(8,128)(2,1)}) %all-gather.16.cloned.1.call-update) | async-done | bytes 8388624 | tf_op jit(solution)/shard_map/all_gather | solution.py:241
  335.0 19.4 fusion.110
  369.3 14.1 convolution_convert_fusion.1
  383.9 31.2 %all-gather.10.cloned.1.call-done = bf16[2048,2048]{1,0:T(8,128)(2,1)} async-done(((bf16[64,2048]{1,0:T(8,128)(2,1)}), bf16[2048,2048]{1,0:T(8,128)(2,1)}) %all-gather.10.cloned.1.call-update) | async-done | bytes 8388624 | tf_op jit(solution)/shard_map/all_gather | solution.py:188
  427.0 163.5 %all-gather.8.cloned.1.call-done = bf16[2048,6144]{1,0:T(8,128)(2,1)} async-done(((bf16[64,6144]{1,0:T(8,128)(2,1)}), bf16[2048,6144]{1,0:T(8,128)(2,1)}) %all-gather.8.cloned.1.call-update) | async-done | bytes 25165840 | tf_op jit(solution)/shard_map/all_gather | solution.py:186
  618.9 53.1 %all-to-all-done.1 = bf16[1,256,16,128]{3,1,0,2:T(8,128)(2,1)} async-done(((bf16[1,256,16,128]{3,1,0,2:T(8,128)(2,1)}), bf16[1,256,16,128]{3,1,0,2:T(8,128)(2,1)}, u32[]{:S(2)}, u32[]{:S(2)}) %all-to-all-start.1) | async-done | bytes 1048608 | tf_op jit(solution)/shard_map/all_to_all | solution.py:219
  679.0 33.3 %all-to-all-done = bf16[1,256,16,128]{3,1,0,2:T(8,128)(2,1)S(1)} async-done(((bf16[1,256,16,128]{3,1,0,2:T(8,128)(2,1)}), bf16[1,256,16,128]{3,1,0,2:T(8,128)(2,1)S(1)}, u32[]{:S(2)}, u32[]{:S(2)}) %all-to-all-start) | async-done | bytes 1048608 | tf_op jit(solution)/shard_map/all_to_all | solution.py:216
  716.6 15.0 convolution_convert_fusion
  745.4 26.7 %while.31 = (s32[]{:T(128)}, bf16[2,1,512,4,128]{4,2,0,3,1:T(8,128)(2,1)}, f32[2,1,4,512]{3,2,1,0:T(4,128)S(1)}, s32[2]{0:T(128)S(1)}, bf16[1,1024,4,128]{3,1,2,...) while((s32[]{:T(128)}, ...), condition=%wide.region_5.6_spmd.clone, body=%wide.region_2.5_spmd.clone.sunk | while | flops 1099955712 | bytes 35199700 | solution.py:81
  773.2 55.0 %while.32 = (s32[]{:T(128)}, f32[1,1024,4,128]{1,3,2,0:T(8,128)S(1)}, f32[1,1024,4,128]{1,3,2,0:T(8,128)}, bf16[2,1,512,4,128]{4,2,0,3,1:T(8,128)(2,1)}, s32[2]{...) while((s32[]{:T(128)}, ...), condition=%wide.region_9.10_spmd.clone, body=%wide.region_7.9_spmd.clone.sunk | while | flops 2709257728 | bytes 170966912 | solution.py:131
  836.5 22.4 %all-to-all-done.5 = bf16[1,1024,4,128]{3,2,0,1:T(4,128)(2,1)S(1)} async-done(((bf16[1,1024,4,128]{3,2,0,1:T(4,128)(2,1)}), bf16[1,1024,4,128]{3,2,0,1:T(4,128)(2,1)S(1)}, u32[]{:S(2)}, u32[]{:S(2)}) %all-to-all-start.5) | async-done | bytes 1048608 | tf_op jit(solution)/shard_map/all_to_all | solution.py:297
  863.5 14.3 convert_bitcast_fusion.1
  900.6 45.7 %all-to-all-done.7 = bf16[1,1024,4,128]{3,2,0,1:T(4,128)(2,1)} async-done(((bf16[1,1024,4,128]{3,2,0,1:T(4,128)(2,1)}), bf16[1,1024,4,128]{3,2,0,1:T(4,128)(2,1)}, u32[]{:S(2)}, u32[]{:S(2)}) %all-to-all-start.7) | async-done | bytes 1048608 | tf_op jit(solution)/shard_map/all_to_all | solution.py:303
  966.1 31.0 %all-to-all-done.3 = bf16[1,1024,4,128]{3,2,0,1:T(4,128)(2,1)S(1)} async-done(((bf16[1,1024,4,128]{3,2,0,1:T(4,128)(2,1)}), bf16[1,1024,4,128]{3,2,0,1:T(4,128)(2,1)S(1)}, u32[]{:S(2)}, u32[]{:S(2)}) %all-to-all-start.3) | async-done | bytes 1048608 | tf_op jit(solution)/shard_map/all_to_all | solution.py:227
  999.8 14.7 fusion.79
  1033.1 21.9 %fusion.103 = f32[2048,6144]{1,0:T(8,128)} fusion(bf16[256,6144]{0,1:T(8,128)(2,1)} %bitcast.282, bf16[1,256,2048]{2,1,0:T(8,128)(2,1)S(1)} %copy-done.4, f32[2048]{0:T(1024)S(1)} %copy-done.31, f32[2048]{0:T(1024)S(1)} %copy-done.29, f32[256]{0:T(256)S(1)} %copy-done.35, f32[256]{0:T(256)S(1)} %copy-done.37), kind=kOutput, calls=%fused_computation.179 | convolution fusion | flops 6445596672 | bytes 54544384 | tf_op jit(solution)/shard_map/dot_general | solution.py:50
  1084.6 62.8 %all-reduce.28.cloned.1.call-done = (f32[6144]{0:T(1024)}, f32[2048]{0:T(1024)}, f32[2048]{0:T(1024)}, f32[2048]{0:T(1024)}, f32[2048]{0:T(1024)}, /*index=5*/f32[2048]{0:T(1024)}) async-done(((f32[6144]{0:T(1024)}, f32[2048]{0:T(1024)}, f32[2048]{0:T(1024)}, f32[2048]{0:T(1024)}, f32[2048]{0:T(1024)}, /*index=5*/f32[2048]{0:T(1024)}), (f32[6144]{0:T(1024)}, f32[2048]{0:T(1024)}, f32[2048]{0:T(1024)}, ...) | async-done | bytes 65552
  1154.5 361.0 %reduce-scatter.13.cloned.1.call-done = f32[64,2048]{1,0:T(8,128)} async-done(((f32[2048,2048]{1,0:T(8,128)}), f32[64,2048]{1,0:T(8,128)}) %reduce-scatter.13.cloned.1.call-update) | async-done | bytes 524304 | tf_op jit(solution)/shard_map/reduce_scatter | solution.py:328
  1515.5 436.4 %reduce-scatter.11.cloned.1.call-done = f32[64,6144]{1,0:T(8,128)} async-done(((f32[2048,6144]{1,0:T(8,128)}), f32[64,6144]{1,0:T(8,128)}) %reduce-scatter.11.cloned.1.call-update) | async-done | bytes 1572880 | tf_op jit(solution)/shard_map/reduce_scatter | solution.py:326
  (299 shorter events, 293.6 us)
Async XLA Ops:
  7.2 135.9 %all-gather.12.cloned.1.call-start = ((), (), s32[]{:S(2)}) async-start(), calls=%async_computation.16 | async-start | bytes 5242880 | tf_op jit(solution)/shard_map/all_gather | solution.py:243
  8.8 581.7 %copy-start.36 = (f32[256]{0:T(256)}, f32[256]{0:T(256)S(1)}, u32[]{:S(2)}) copy-start(f32[256]{0:T(256)S(1)} %broadcast_multiply_fusion.1) | copy-start | bytes 3076
  10.5 580.0 %copy-start.34 = (f32[256]{0:T(256)}, f32[256]{0:T(256)S(1)}, u32[]{:S(2)}) copy-start(f32[256]{0:T(256)S(1)} %fusion.101) | copy-start | bytes 3076
  62.4 135.5 %all-gather.14.cloned.1.call-start = ((), (), s32[]{:S(2)}) async-start(), calls=%async_computation.17 | async-start | bytes 9437184 | tf_op jit(solution)/shard_map/all_gather | solution.py:239
  63.1 217.1 %all-gather.18.cloned.1.call-start = ((), (), s32[]{:S(2)}) async-start(), calls=%async_computation.20 | async-start | bytes 5242880 | tf_op jit(solution)/shard_map/all_gather | solution.py:254
  65.1 269.8 %all-gather.16.cloned.1.call-start = ((), (), s32[]{:S(2)}) async-start(), calls=%async_computation.18 | async-start | bytes 9437184 | tf_op jit(solution)/shard_map/all_gather | solution.py:241
  65.7 349.3 %all-gather.10.cloned.1.call-start = ((), (), s32[]{:S(2)}) async-start(), calls=%async_computation.15 | async-start | bytes 8650752 | tf_op jit(solution)/shard_map/all_gather | solution.py:188
  66.3 524.2 %all-gather.8.cloned.1.call-start = ((), (), s32[]{:S(2)}) async-start(), calls=%async_computation.14 | async-start | bytes 25952256 | tf_op jit(solution)/shard_map/all_gather | solution.py:186
  66.9 932.8 %reduce-scatter.9.cloned.1.call-start = ((), (), s32[]{:S(2)}) async-start(), calls=%async_computation.21 | async-start | bytes 5242880 | tf_op jit(solution)/shard_map/reduce_scatter | solution.py:260
  369.2 702.3 %reduce-scatter.15.cloned.1.call-start = ((), (), s32[]{:S(2)}) async-start(), calls=%async_computation.24 | async-start | bytes 9437184 | tf_op jit(solution)/shard_map/reduce_scatter | solution.py:267
  422.3 190.5 %all-to-all-start.4 = ((bf16[1,256,16,128]{3,1,0,2:T(8,128)(2,1)}), bf16[1,256,16,128]{3,1,0,2:T(8,128)(2,1)}, u32[]{:S(2)}, u32[]{:S(2)}) async-start(bf16[1,256,16,128]{3,1,0,2:T(8,128)(2,1)} %copy.146), calls=%async_computation.5 | async-start | bytes 2097152 | tf_op jit(solution)/shard_map/all_to_all | solution.py:286
  612.8 59.3 %all-to-all-start.1 = ((bf16[1,256,16,128]{3,1,0,2:T(8,128)(2,1)}), bf16[1,256,16,128]{3,1,0,2:T(8,128)(2,1)}, u32[]{:S(2)}, u32[]{:S(2)}) async-start(bf16[1,256,16,128]{3,1,0,2:T(8,128)(2,1)} %maximum_bitcast_fusion.1), calls=%async_computation.1 | async-start | bytes 2097152 | tf_op jit(solution)/shard_map/all_to_all | solution.py:219
  672.0 40.2 %all-to-all-start = ((bf16[1,256,16,128]{3,1,0,2:T(8,128)(2,1)}), bf16[1,256,16,128]{3,1,0,2:T(8,128)(2,1)S(1)}, u32[]{:S(2)}, u32[]{:S(2)}) async-start(bf16[1,256,16,128]{3,1,0,2:T(8,128)(2,1)} %maximum_bitcast_fusion), calls=%async_computation | async-start | bytes 2097152 | tf_op jit(solution)/shard_map/all_to_all | solution.py:216
  712.3 29.8 %all-to-all-start.2 = ((bf16[1,256,16,128]{3,1,0,2:T(8,128)(2,1)}), bf16[1,256,16,128]{3,1,0,2:T(8,128)(2,1)}, u32[]{:S(2)}, u32[]{:S(2)}) async-start(bf16[1,256,16,128]{3,1,0,2:T(8,128)(2,1)} %bitcast.288), calls=%async_computation.2 | async-start | bytes 2097152 | tf_op jit(solution)/shard_map/all_to_all | solution.py:222
  716.5 357.7 %reduce-scatter.17.cloned.1.call-start = ((), (), s32[]{:S(2)}) async-start(), calls=%async_computation.25 | async-start | bytes 9437184 | tf_op jit(solution)/shard_map/reduce_scatter | solution.py:273
  831.3 27.6 %all-to-all-start.5 = ((bf16[1,1024,4,128]{3,2,0,1:T(4,128)(2,1)}), bf16[1,1024,4,128]{3,2,0,1:T(4,128)(2,1)S(1)}, u32[]{:S(2)}, u32[]{:S(2)}) async-start(bf16[1,1024,4,128]{3,2,0,1:T(4,128)(2,1)} %copy.149), calls=%async_computation.6 | async-start | bytes 2097152 | tf_op jit(solution)/shard_map/all_to_all | solution.py:297
  859.9 28.8 %all-to-all-start.6 = ((bf16[1,1024,4,128]{3,2,0,1:T(4,128)(2,1)}), bf16[1,1024,4,128]{3,2,0,1:T(4,128)(2,1)S(1)}, u32[]{:S(2)}, u32[]{:S(2)}) async-start(bf16[1,1024,4,128]{3,2,0,1:T(4,128)(2,1)} %copy.152), calls=%async_computation.7 | async-start | bytes 2097152 | tf_op jit(solution)/shard_map/all_to_all | solution.py:300
  863.4 213.6 %reduce-scatter.7.cloned.1.call-start = ((), (), s32[]{:S(2)}) async-start(), calls=%async_computation.19 | async-start | bytes 5242880 | tf_op jit(solution)/shard_map/reduce_scatter | solution.py:247
  888.6 57.6 %all-to-all-start.7 = ((bf16[1,1024,4,128]{3,2,0,1:T(4,128)(2,1)}), bf16[1,1024,4,128]{3,2,0,1:T(4,128)(2,1)}, u32[]{:S(2)}, u32[]{:S(2)}) async-start(bf16[1,1024,4,128]{3,2,0,1:T(4,128)(2,1)} %copy.154), calls=%async_computation.8 | async-start | bytes 2097152 | tf_op jit(solution)/shard_map/all_to_all | solution.py:303
  946.3 50.8 %all-to-all-start.3 = ((bf16[1,1024,4,128]{3,2,0,1:T(4,128)(2,1)}), bf16[1,1024,4,128]{3,2,0,1:T(4,128)(2,1)S(1)}, u32[]{:S(2)}, u32[]{:S(2)}) async-start(bf16[1,1024,4,128]{3,2,0,1:T(4,128)(2,1)} %copy.143), calls=%async_computation.3 | async-start | bytes 2097152 | tf_op jit(solution)/shard_map/all_to_all | solution.py:227
  950.2 197.1 %all-reduce.28.cloned.1.call-start = ((), (), s32[]{:S(2)}) async-start(), calls=%async_computation.26 | async-start | bytes 131072
  1024.2 491.2 %reduce-scatter.13.cloned.1.call-start = ((), (), s32[]{:S(2)}) async-start(), calls=%async_computation.23 | async-start | bytes 17301504 | tf_op jit(solution)/shard_map/reduce_scatter | solution.py:328
  1032.4 919.5 %reduce-scatter.11.cloned.1.call-start = ((), (), s32[]{:S(2)}) async-start(), calls=%async_computation.22 | async-start | bytes 51904512 | tf_op jit(solution)/shard_map/reduce_scatter | solution.py:326
  1148.1 804.3 %copy-start.47 = (f32[64]{0:T(128)}, f32[64]{0:T(128)S(1)}, u32[]{:S(2)}) copy-start(f32[64]{0:T(128)S(1)} %dynamic-slice.16) | copy-start | bytes 772
  (52 other events, 1554.9 us)
Sparse Core Ops, SparseCore 0:
  62.5 80.5 all-gather.11
  144.9 52.9 all-gather.13
  199.5 80.7 all-gather.17
  282.0 52.9 all-gather.15
  337.7 77.2 all-gather.9
  417.8 172.6 all-gather.7
  592.8 99.6 reduce-scatter.8
  696.4 88.4 reduce-scatter.14
  788.3 71.2 reduce-scatter.16
  877.9 111.9 reduce-scatter.6
  1024.4 122.9 all-reduce.27
  1150.1 365.3 reduce-scatter.12
  1522.5 429.3 reduce-scatter.10
where the time goes:
time: 1960 us
  waiting for transfers between devices  1480 us (76%)
  matrix products  222 us (11%)
  local copies, waits for them, and re-layouts  76 us (4%)
  blocking collectives  66.9 us (3%)
  other arithmetic  53.9 us (3%)
  starting transfers between devices  32.8 us (2%)
    reduce_scatter x1, waiting for transfers between devices, local(): lax.psum_scatter(in_delta, ('fsdp', 'seq'), scatter_dimension=0, tiled=True)  436 us
    reduce_scatter x1, waiting for transfers between devices, local(): lax.psum_scatter(out_delta, ('fsdp', 'seq'), scatter_dimension=0, tiled=T...  361 us
    all_gather x1, waiting for transfers between devices, local(): lax.all_gather(in_weight, ('fsdp', 'seq'), axis=0, tiled=True)  164 us
    dot_general x4, matrix products, times_transposed(): lax.dot_general(left_side, right_side, (((1,), (1,)), ((), ())), preferre...  71.4 us
    all_gather x1, waiting for transfers between devices, local(): lax.all_gather(second_in, 'seq', axis=1, tiled=True)  66.3 us
    unnamed x14, waiting for transfers between devices  65.2 us
    dot_general x4, matrix products, transposed_times(): lax.dot_general(left_side, right_side, (((0,), (0,)), ((), ())), preferre...  59.1 us
    unnamed x2, blocking collectives  57.1 us
  transfers between devices with their start and end apart: 21, of which 16 were waited for; matrix products, arithmetic and copies ran while one was open for 16% of the time, Pallas kernels for 0%

commit v1 on v0

--- a/solution.py
+++ b/solution.py
@@ -8,6 +8,28 @@
 ROT = 32
 EPSILON = 1e-05
 MASKED_SCORE = -1e30
+
+
+def split_up(value, dim, size):
+    before, after = (value.shape[:dim], value.shape[dim + 1 :])
+    return jnp.moveaxis(value.reshape(*before, size, -1, *after), dim, 0)
+
+
+def in_order(tiles, dim):
+    tiles = jnp.moveaxis(tiles, 0, dim)
+    shape = tiles.shape
+    return tiles.reshape(*shape[:dim], shape[dim] * shape[dim + 1], *shape[dim + 2 :])
+
+
+def swapped_with_each(value, axis, split_dim, concat_dim):
+    size, place = (lax.axis_size(axis), lax.axis_index(axis))
+    parts = split_up(value, split_dim, size)
+    finished = [parts[place]]
+    for lap in range(1, size):
+        sent = parts[place ^ lap]
+        finished.append(lax.ppermute(sent, axis, [(i, i ^ lap) for i in range(size)]))
+    parts = jnp.stack(finished)[place ^ jnp.arange(size)]
+    return in_order(parts, concat_dim)
 
 
 def layer_norm(values, norm_gain, norm_shift):
@@ -216,9 +238,7 @@
         lax.all_to_all(
             turned[0].astype(jnp.bfloat16), "seq", split_axis=2, concat_axis=1, tiled=True
         ),
-        lax.all_to_all(
-            turned[1].astype(jnp.bfloat16), "seq", split_axis=2, concat_axis=1, tiled=True
-        ),
+        swapped_with_each(turned[1].astype(jnp.bfloat16), "seq", 2, 1),
         lax.all_to_all(
             joined[:, :, 2].astype(jnp.bfloat16), "seq", split_axis=2, concat_axis=1, tiled=True
         ),

time: 1960 us -> 1960 us (level)
    all_to_all x1 -> x0, waiting for transfers between devices: 53.1 us -> none  [local(): lax.all_to_all(turned[1].astype(jnp.bfloat16), 'seq', split_axis=2, conca...]
  transfers between devices with their start and end apart: 21 -> 23, of which waited for: 16 -> 16; matrix products, arithmetic and copies ran while one was open for 16% -> 17% of each run, Pallas kernels for 0% -> 0%
where the time goes in v1:
time: 1960 us; the launch traced here: 1950 us
  waiting for transfers between devices  1470 us (75%)
  matrix products  222 us (11%)
  local copies, waits for them, and re-layouts  82 us (4%)
  blocking collectives  66.9 us (3%)
  other arithmetic  55.1 us (3%)
  starting transfers between devices  34.2 us (2%)
    reduce_scatter x1, waiting for transfers between devices, local(): lax.psum_scatter(in_delta, ('fsdp', 'seq'), scatter_dimension=0, tiled=True)  437 us
    reduce_scatter x1, waiting for transfers between devices, local(): lax.psum_scatter(out_delta, ('fsdp', 'seq'), scatter_dimension=0, tiled=T...  361 us
    all_gather x1, waiting for transfers between devices, local(): lax.all_gather(in_weight, ('fsdp', 'seq'), axis=0, tiled=True)  164 us
    dot_general x4, matrix products, times_transposed(): lax.dot_general(left_side, right_side, (((1,), (1,)), ((), ())), preferre...  71.4 us
    all_gather x1, waiting for transfers between devices, local(): lax.all_gather(second_in, 'seq', axis=1, tiled=True)  66.3 us
    unnamed x14, waiting for transfers between devices  63.3 us
    dot_general x4, matrix products, transposed_times(): lax.dot_general(left_side, right_side, (((0,), (0,)), ((), ())), preferre...  58.4 us
    unnamed x2, blocking collectives  57.2 us
  transfers between devices with their start and end apart: 23, of which 16 were waited for; matrix products, arithmetic and copies ran while one was open for 17% of the time, Pallas kernels for 0%

profile of v1, /device:TPU:0, one launch (start us, length us, event | category | flops | bytes accessed | tf_op | source)
XLA Modules:
  0.0 1954.5 jit_solution(7566001488589176065)
XLA Ops:
  16.4 43.2 %all-reduce.25 = (bf16[6144]{0:T(1024)(128)(2,1)S(1)}, bf16[2048]{0:T(1024)(128)(2,1)S(1)}, bf16[2048]{0:T(1024)(128)(2,1)S(1)}, bf16[2048]{0:T(1024)(128)(2,1)S...) all-reduce(bf16[6144]{0:T(1024)(128)(2,1)S(1)} %dynamic-update-slic, ...), channel_id=1, replica_groups=mesh['fsdp'=8,'seq'=4] {'fsdp','seq'}, use_global_device_ids=true, to_apply=%add.12 | all-reduce | flops 18432 | bytes 73728
  76.7 66.3 %all-gather.12.cloned.1.call-done = bf16[1,1024,2048]{2,1,0:T(8,128)(2,1)} async-done(((bf16[1,256,2048]{2,1,0:T(8,128)(2,1)}), bf16[1,1024,2048]{2,1,0:T(8,128)(2,1)}) %all-gather.12.cloned.1.call-update) | async-done | bytes 4194320 | tf_op jit(solution)/shard_map/all_gather | solution.py:263
  143.0 54.8 %all-gather.14.cloned.1.call-done = bf16[2048,2048]{1,0:T(8,128)(2,1)} async-done(((bf16[256,2048]{1,0:T(8,128)(2,1)}), bf16[2048,2048]{1,0:T(8,128)(2,1)}) %all-gather.14.cloned.1.call-update) | async-done | bytes 8388624 | tf_op jit(solution)/shard_map/all_gather | solution.py:259
  197.9 31.6 %multiply_convert_fusion.1 = (bf16[1024,2048]{1,0:T(8,128)(2,1)}, f32[1024,2048]{1,0:T(8,128)}, f32[1024,2048]{1,0:T(8,128)}) fusion(f32[2048]{0:T(1024)S(1)} %bitcast.314, bf16[2048,2048]{1,0:T(8,128)(2,1)} %all-gather.14.cloned.1.call-done, bf16[1,1024,2048]{2,1,0:T(8,128)(2,1)} %all-gather.12.cloned.1.call-done), kind=kOutput, calls=%fused_computation.62 | convolution fusion | flops 8728346624 | bytes 33562624 | tf_op jit(solution)/shard_map/dot_general | solution.py:66
  229.4 50.8 %all-gather.18.cloned.1.call-done = bf16[1,1024,2048]{2,1,0:T(8,128)(2,1)} async-done(((bf16[1,256,2048]{2,1,0:T(8,128)(2,1)}), bf16[1,1024,2048]{2,1,0:T(8,128)(2,1)}) %all-gather.18.cloned.1.call-update) | async-done | bytes 4194320 | tf_op jit(solution)/shard_map/all_gather | solution.py:274
  280.3 54.7 %all-gather.16.cloned.1.call-done = bf16[2048,2048]{1,0:T(8,128)(2,1)} async-done(((bf16[256,2048]{1,0:T(8,128)(2,1)}), bf16[2048,2048]{1,0:T(8,128)(2,1)}) %all-gather.16.cloned.1.call-update) | async-done | bytes 8388624 | tf_op jit(solution)/shard_map/all_gather | solution.py:261
  335.0 19.4 fusion.119
  383.8 31.2 %all-gather.10.cloned.1.call-done = bf16[2048,2048]{1,0:T(8,128)(2,1)} async-done(((bf16[64,2048]{1,0:T(8,128)(2,1)}), bf16[2048,2048]{1,0:T(8,128)(2,1)}) %all-gather.10.cloned.1.call-update) | async-done | bytes 8388624 | tf_op jit(solution)/shard_map/all_gather | solution.py:210
  426.9 163.6 %all-gather.8.cloned.1.call-done = bf16[2048,6144]{1,0:T(8,128)(2,1)} async-done(((bf16[64,6144]{1,0:T(8,128)(2,1)}), bf16[2048,6144]{1,0:T(8,128)(2,1)}) %all-gather.8.cloned.1.call-update) | async-done | bytes 25165840 | tf_op jit(solution)/shard_map/all_gather | solution.py:208
  628.0 38.7 %all-to-all-done = bf16[1,256,16,128]{3,1,0,2:T(8,128)(2,1)} async-done(((bf16[1,256,16,128]{3,1,0,2:T(8,128)(2,1)}), bf16[1,256,16,128]{3,1,0,2:T(8,128)(2,1)}, u32[]{:S(2)}, u32[]{:S(2)}) %all-to-all-start) | async-done | bytes 1048608 | tf_op jit(solution)/shard_map/all_to_all | solution.py:238
  672.3 14.3 convolution_convert_fusion
  688.9 14.3 collective-permute-done.1
  710.5 24.4 %all-to-all-done.1 = bf16[1,256,16,128]{3,1,0,2:T(8,128)(2,1)} async-done(((bf16[1,256,16,128]{3,1,0,2:T(8,128)(2,1)}), bf16[1,256,16,128]{3,1,0,2:T(8,128)(2,1)}, u32[]{:S(2)}, u32[]{:S(2)}) %all-to-all-start.1) | async-done | bytes 1048608 | tf_op jit(solution)/shard_map/all_to_all | solution.py:242
  738.2 26.9 %while.31 = (s32[]{:T(128)}, bf16[2,1,512,4,128]{4,2,0,3,1:T(8,128)(2,1)}, f32[2,1,4,512]{3,2,1,0:T(4,128)S(1)}, s32[2]{0:T(128)S(1)}, bf16[1,1024,4,128]{3,1,2,...) while((s32[]{:T(128)}, ...), condition=%wide.region_5.6_spmd.clone, body=%wide.region_2.5_spmd.clone.sunk | while | flops 1099955712 | bytes 35199700 | solution.py:103
  766.2 56.2 %while.32 = (s32[]{:T(128)}, f32[1,1024,4,128]{1,3,2,0:T(8,128)S(1)}, f32[1,1024,4,128]{1,3,2,0:T(8,128)}, bf16[2,1,512,4,128]{4,2,0,3,1:T(8,128)(2,1)}, s32[2]{...) while((s32[]{:T(128)}, ...), condition=%wide.region_9.10_spmd.clone, body=%wide.region_7.9_spmd.clone.sunk | while | flops 2709257728 | bytes 170966912 | solution.py:153
  830.6 24.3 %all-to-all-done.4 = bf16[1,1024,4,128]{3,2,0,1:T(4,128)(2,1)S(1)} async-done(((bf16[1,1024,4,128]{3,2,0,1:T(4,128)(2,1)}), bf16[1,1024,4,128]{3,2,0,1:T(4,128)(2,1)S(1)}, u32[]{:S(2)}, u32[]{:S(2)}) %all-to-all-start.4) | async-done | bytes 1048608 | tf_op jit(solution)/shard_map/all_to_all | solution.py:317
  859.5 14.4 convert_bitcast_fusion.1
  896.6 46.3 %all-to-all-done.6 = bf16[1,1024,4,128]{3,2,0,1:T(4,128)(2,1)} async-done(((bf16[1,1024,4,128]{3,2,0,1:T(4,128)(2,1)}), bf16[1,1024,4,128]{3,2,0,1:T(4,128)(2,1)}, u32[]{:S(2)}, u32[]{:S(2)}) %all-to-all-start.6) | async-done | bytes 1048608 | tf_op jit(solution)/shard_map/all_to_all | solution.py:323
  962.4 31.7 %all-to-all-done.2 = bf16[1,1024,4,128]{3,2,0,1:T(4,128)(2,1)S(1)} async-done(((bf16[1,1024,4,128]{3,2,0,1:T(4,128)(2,1)}), bf16[1,1024,4,128]{3,2,0,1:T(4,128)(2,1)S(1)}, u32[]{:S(2)}, u32[]{:S(2)}) %all-to-all-start.2) | async-done | bytes 1048608 | tf_op jit(solution)/shard_map/all_to_all | solution.py:247
  996.8 14.7 fusion.79
  1030.1 21.9 %fusion.112 = f32[2048,6144]{1,0:T(8,128)} fusion(bf16[256,6144]{0,1:T(8,128)(2,1)} %bitcast.294, bf16[1,256,2048]{2,1,0:T(8,128)(2,1)S(1)} %copy-done.4, f32[2048]{0:T(1024)S(1)} %copy-done.33, f32[2048]{0:T(1024)S(1)} %copy-done.28, f32[256]{0:T(256)S(1)} %copy-done.37, f32[256]{0:T(256)S(1)} %copy-done.39), kind=kOutput, calls=%fused_computation.199 | convolution fusion | flops 6445596672 | bytes 54544384 | tf_op jit(solution)/shard_map/dot_general | solution.py:72
  1081.6 60.9 %all-reduce.28.cloned.1.call-done = (f32[6144]{0:T(1024)}, f32[2048]{0:T(1024)}, f32[2048]{0:T(1024)}, f32[2048]{0:T(1024)}, f32[2048]{0:T(1024)}, /*index=5*/f32[2048]{0:T(1024)}) async-done(((f32[6144]{0:T(1024)}, f32[2048]{0:T(1024)}, f32[2048]{0:T(1024)}, f32[2048]{0:T(1024)}, f32[2048]{0:T(1024)}, /*index=5*/f32[2048]{0:T(1024)}), (f32[6144]{0:T(1024)}, f32[2048]{0:T(1024)}, f32[2048]{0:T(1024)}, ...) | async-done | bytes 65552
  1149.6 361.0 %reduce-scatter.13.cloned.1.call-done = f32[64,2048]{1,0:T(8,128)} async-done(((f32[2048,2048]{1,0:T(8,128)}), f32[64,2048]{1,0:T(8,128)}) %reduce-scatter.13.cloned.1.call-update) | async-done | bytes 524304 | tf_op jit(solution)/shard_map/reduce_scatter | solution.py:348
  1510.6 436.6 %reduce-scatter.11.cloned.1.call-done = f32[64,6144]{1,0:T(8,128)} async-done(((f32[2048,6144]{1,0:T(8,128)}), f32[64,6144]{1,0:T(8,128)}) %reduce-scatter.11.cloned.1.call-update) | async-done | bytes 1572880 | tf_op jit(solution)/shard_map/reduce_scatter | solution.py:346
  (311 shorter events, 310.9 us)
Async XLA Ops:
  7.2 135.9 %all-gather.12.cloned.1.call-start = ((), (), s32[]{:S(2)}) async-start(), calls=%async_computation.15 | async-start | bytes 5242880 | tf_op jit(solution)/shard_map/all_gather | solution.py:263
  62.4 135.5 %all-gather.14.cloned.1.call-start = ((), (), s32[]{:S(2)}) async-start(), calls=%async_computation.16 | async-start | bytes 9437184 | tf_op jit(solution)/shard_map/all_gather | solution.py:259
  63.1 217.1 %all-gather.18.cloned.1.call-start = ((), (), s32[]{:S(2)}) async-start(), calls=%async_computation.19 | async-start | bytes 5242880 | tf_op jit(solution)/shard_map/all_gather | solution.py:274
  65.1 269.8 %all-gather.16.cloned.1.call-start = ((), (), s32[]{:S(2)}) async-start(), calls=%async_computation.17 | async-start | bytes 9437184 | tf_op jit(solution)/shard_map/all_gather | solution.py:261
  65.7 349.3 %all-gather.10.cloned.1.call-start = ((), (), s32[]{:S(2)}) async-start(), calls=%async_computation.14 | async-start | bytes 8650752 | tf_op jit(solution)/shard_map/all_gather | solution.py:210
  66.3 524.2 %all-gather.8.cloned.1.call-start = ((), (), s32[]{:S(2)}) async-start(), calls=%async_computation.13 | async-start | bytes 25952256 | tf_op jit(solution)/shard_map/all_gather | solution.py:208
  66.9 929.9 %reduce-scatter.9.cloned.1.call-start = ((), (), s32[]{:S(2)}) async-start(), calls=%async_computation.20 | async-start | bytes 5242880 | tf_op jit(solution)/shard_map/reduce_scatter | solution.py:280
  369.2 699.3 %reduce-scatter.15.cloned.1.call-start = ((), (), s32[]{:S(2)}) async-start(), calls=%async_computation.23 | async-start | bytes 9437184 | tf_op jit(solution)/shard_map/reduce_scatter | solution.py:287
  422.3 190.6 %all-to-all-start.3 = ((bf16[1,256,16,128]{3,1,0,2:T(8,128)(2,1)}), bf16[1,256,16,128]{3,1,0,2:T(8,128)(2,1)}, u32[]{:S(2)}, u32[]{:S(2)}) async-start(bf16[1,256,16,128]{3,1,0,2:T(8,128)(2,1)} %copy.143), calls=%async_computation.4 | async-start | bytes 2097152 | tf_op jit(solution)/shard_map/all_to_all | solution.py:306
  612.8 53.9 %all-to-all-start = ((bf16[1,256,16,128]{3,1,0,2:T(8,128)(2,1)}), bf16[1,256,16,128]{3,1,0,2:T(8,128)(2,1)}, u32[]{:S(2)}, u32[]{:S(2)}) async-start(bf16[1,256,16,128]{3,1,0,2:T(8,128)(2,1)} %maximum_bitcast_fusion), calls=%async_computation | async-start | bytes 2097152 | tf_op jit(solution)/shard_map/all_to_all | solution.py:238
  622.4 66.5 %collective-permute-start = (bf16[1,256,4,128]{3,1,2,0:T(8,128)(2,1)}, bf16[1,256,4,128]{3,1,2,0:T(8,128)(2,1)S(1)}, u32[]{:S(2)}, u32[]{:S(2)}) collective-permute-start(bf16[1,256,4,128]{3,1,2,0:T(8,128)(2,1)} %get-tuple-element.302), channel_id=1, source_target_pairs={{0,1},{1,0},{2,3},{3,2},{4,5},{5,4},{6,7},{7,6},{8,9},{9,8},{10,11... | collective-permute-start | bytes 786440 | tf_op jit(solution)/shard_map/ppermute | solution.py:30
  624.3 78.9 %collective-permute-start.1 = (bf16[1,256,4,128]{3,1,2,0:T(8,128)(2,1)}, bf16[1,256,4,128]{3,1,2,0:T(8,128)(2,1)S(1)}, u32[]{:S(2)}, u32[]{:S(2)}) collective-permute-start(bf16[1,256,4,128]{3,1,2,0:T(8,128)(2,1)} %get-tuple-element.303), channel_id=1, source_target_pairs={{0,2},{1,3},{2,0},{3,1},{4,6},{5,7},{6,4},{7,5},{8,10},{9,11},{10,... | collective-permute-start | bytes 786440 | tf_op jit(solution)/shard_map/ppermute | solution.py:30
  626.7 76.5 %collective-permute-start.2 = (bf16[1,256,4,128]{3,1,2,0:T(8,128)(2,1)}, bf16[1,256,4,128]{3,1,2,0:T(8,128)(2,1)S(1)}, u32[]{:S(2)}, u32[]{:S(2)}) collective-permute-start(bf16[1,256,4,128]{3,1,2,0:T(8,128)(2,1)} %get-tuple-element.304), channel_id=1, source_target_pairs={{0,3},{1,2},{2,1},{3,0},{4,7},{5,6},{6,5},{7,4},{8,11},{9,10},{10,... | collective-permute-start | bytes 786440 | tf_op jit(solution)/shard_map/ppermute | solution.py:30
  666.7 68.1 %all-to-all-start.1 = ((bf16[1,256,16,128]{3,1,0,2:T(8,128)(2,1)}), bf16[1,256,16,128]{3,1,0,2:T(8,128)(2,1)}, u32[]{:S(2)}, u32[]{:S(2)}) async-start(bf16[1,256,16,128]{3,1,0,2:T(8,128)(2,1)} %bitcast.221), calls=%async_computation.1 | async-start | bytes 2097152 | tf_op jit(solution)/shard_map/all_to_all | solution.py:242
  672.3 399.0 %reduce-scatter.17.cloned.1.call-start = ((), (), s32[]{:S(2)}) async-start(), calls=%async_computation.24 | async-start | bytes 9437184 | tf_op jit(solution)/shard_map/reduce_scatter | solution.py:293
  825.4 29.5 %all-to-all-start.4 = ((bf16[1,1024,4,128]{3,2,0,1:T(4,128)(2,1)}), bf16[1,1024,4,128]{3,2,0,1:T(4,128)(2,1)S(1)}, u32[]{:S(2)}, u32[]{:S(2)}) async-start(bf16[1,1024,4,128]{3,2,0,1:T(4,128)(2,1)} %copy.146), calls=%async_computation.5 | async-start | bytes 2097152 | tf_op jit(solution)/shard_map/all_to_all | solution.py:317
  855.9 28.8 %all-to-all-start.5 = ((bf16[1,1024,4,128]{3,2,0,1:T(4,128)(2,1)}), bf16[1,1024,4,128]{3,2,0,1:T(4,128)(2,1)S(1)}, u32[]{:S(2)}, u32[]{:S(2)}) async-start(bf16[1,1024,4,128]{3,2,0,1:T(4,128)(2,1)} %copy.149), calls=%async_computation.6 | async-start | bytes 2097152 | tf_op jit(solution)/shard_map/all_to_all | solution.py:320
  859.4 214.6 %reduce-scatter.7.cloned.1.call-start = ((), (), s32[]{:S(2)}) async-start(), calls=%async_computation.18 | async-start | bytes 5242880 | tf_op jit(solution)/shard_map/reduce_scatter | solution.py:267
  884.7 58.3 %all-to-all-start.6 = ((bf16[1,1024,4,128]{3,2,0,1:T(4,128)(2,1)}), bf16[1,1024,4,128]{3,2,0,1:T(4,128)(2,1)}, u32[]{:S(2)}, u32[]{:S(2)}) async-start(bf16[1,1024,4,128]{3,2,0,1:T(4,128)(2,1)} %copy.151), calls=%async_computation.7 | async-start | bytes 2097152 | tf_op jit(solution)/shard_map/all_to_all | solution.py:323
  942.9 51.2 %all-to-all-start.2 = ((bf16[1,1024,4,128]{3,2,0,1:T(4,128)(2,1)}), bf16[1,1024,4,128]{3,2,0,1:T(4,128)(2,1)S(1)}, u32[]{:S(2)}, u32[]{:S(2)}) async-start(bf16[1,1024,4,128]{3,2,0,1:T(4,128)(2,1)} %copy.140), calls=%async_computation.2 | async-start | bytes 2097152 | tf_op jit(solution)/shard_map/all_to_all | solution.py:247
  946.5 196.0 %all-reduce.28.cloned.1.call-start = ((), (), s32[]{:S(2)}) async-start(), calls=%async_computation.25 | async-start | bytes 131072
  1021.2 489.4 %reduce-scatter.13.cloned.1.call-start = ((), (), s32[]{:S(2)}) async-start(), calls=%async_computation.22 | async-start | bytes 17301504 | tf_op jit(solution)/shard_map/reduce_scatter | solution.py:348
  1029.4 917.8 %reduce-scatter.11.cloned.1.call-start = ((), (), s32[]{:S(2)}) async-start(), calls=%async_computation.21 | async-start | bytes 51904512 | tf_op jit(solution)/shard_map/reduce_scatter | solution.py:346
  1143.3 804.5 %copy-start.49 = (f32[64]{0:T(128)}, f32[64]{0:T(128)S(1)}, u32[]{:S(2)}) copy-start(f32[64]{0:T(128)S(1)} %dynamic-slice.32) | copy-start | bytes 772
  (56 other events, 2717.3 us)
Sparse Core Ops, SparseCore 0:
  62.5 80.5 all-gather.11
  144.9 52.9 all-gather.13
  199.5 80.7 all-gather.17
  282.0 52.9 all-gather.15
  337.7 77.2 all-gather.9
  417.8 172.6 all-gather.7
  592.8 119.8 reduce-scatter.8
  716.6 83.4 reduce-scatter.14
  803.6 71.2 reduce-scatter.16
  877.1 109.9 reduce-scatter.6
  1021.4 121.0 all-reduce.27
  1145.2 365.3 reduce-scatter.12
  1517.6 429.5 reduce-scatter.10
